TPU v7x, 32 devices: a whole 2x2x4 slice. The times are simulated.
32 devices in a mesh: dp: 8 (over y, x, core), mp: 4 (over z).
Axes of the slice: x: 2, y: 2, z: 4, core: 2. Of those that a mesh axis runs over, the one named last changes fastest.
Arguments:
- hidden_in: bfloat16 [16384, 2048], P('dp', 'mp')
- positions: int32 [16384], P('dp'), may hold values from 0 to 1023, as said below
- head_counts: int32 [4], replicated, may hold values from 4 to 6, as said below
- attention_gain: float32 [2048], P('mp'), may hold values from 0.5 to 1.5
- query_projection_weight: bfloat16 [2048, 1536], P(None, 'mp'), may hold values from -0.125 to 0.125
- key_weight: bfloat16 [2048, 320], replicated, may hold values from -0.125 to 0.125
- value_weight: bfloat16 [2048, 320], replicated, may hold values from -0.125 to 0.125
- query_gain: float32 [64], replicated, may hold values from 0.25 to 1.75
- key_gain: float32 [64], replicated, may hold values from 0.25 to 1.75
- output_weight: bfloat16 [1536, 2048], P(None, 'mp'), may hold values from -0.75 to 0.75
- feedforward_gain: float32 [2048], P('mp'), may hold values from 0.5 to 1.5
- gate_weight: bfloat16 [2048, 4096], P(None, 'mp'), may hold values from -0.125 to 0.125
- up_weight: bfloat16 [2048, 4096], P(None, 'mp'), may hold values from -0.125 to 0.125
- down_projection_weight: bfloat16 [4096, 2048], P('mp'), may hold values from -0.125 to 0.125
- cotangent: bfloat16 [16384, 2048], P('dp', 'mp'), may hold values from -6 to 6
Outputs:
- output: bfloat16 [16384, 2048], P('dp', 'mp')
- input_gradient: float32 [16384, 2048], P('dp', 'mp')
- attention_gain_gradient: float32 [2048], P('mp')
- query_weight_gradient: float32 [2048, 1536], P(None, 'mp')
- key_weight_gradient: float32 [2048, 320], replicated
- value_weight_gradient: float32 [2048, 320], replicated
- query_gain_gradient: float32 [64], replicated
- key_gain_gradient: float32 [64], replicated
- output_projection_gradient: float32 [1536, 2048], P(None, 'mp')
- feedforward_gain_gradient: float32 [2048], P('mp')
- gate_weight_gradient: float32 [2048, 4096], P(None, 'mp')
- up_weight_gradient: float32 [2048, 4096], P(None, 'mp')
- down_weight_gradient: float32 [4096, 2048], P('mp')
Inputs may be any that keep to these rules, and one draw needn't show every extreme that they name: `head_counts`: the counts sum to 20; index m's live heads follow those of lower indices; the largest count is 6 in every draw. `positions`: position ids count up by one along each sequence of 1024 tokens and restart at zero at its start and at up to three points inside it; the first sequence of all has no restart inside it.
All inputs are finite; a program needn't handle non-finite values.
Results may differ from a plain program's by a relative error of at most 0.025.
Values may be sent and summed in bfloat16 or wider, within the bound.
No kernel may reach another device: no remote copies, remote signals or barrier semaphores. Data moves between devices by JAX's collectives and lax.ppermute only.
A program may use at most 256 MiB of HBM per device.

v0:
```python
import math
import jax
import jax.numpy as jnp
from jax import lax
from jax.sharding import PartitionSpec as P

D = 2048
QH = 20
KVH = 5
HD = 64
LEN = 1024
BLK = 512
NBLK = 2
epsilon = 1e-05
rope_base = 10000.0
masked_score = -1e30


def rotary_tables(positions):
    half = HD // 2
    inverse = jnp.exp(-math.log(rope_base) * (2.0 * jnp.arange(half, dtype=jnp.float32)) / HD)
    angles = positions.astype(jnp.float32)[..., None] * inverse
    angles = jnp.concatenate([angles, angles], axis=-1)
    return (jnp.cos(angles), jnp.sin(angles))


def rotate(vectors, cosine, sine):
    half = vectors.shape[-1] // 2
    turned = jnp.concatenate([-vectors[..., half:], vectors[..., :half]], axis=-1)
    return vectors * cosine + turned * sine


def head_norm(vectors, gain):
    return vectors * lax.rsqrt(jnp.mean(vectors * vectors, axis=-1, keepdims=True) + epsilon) * gain


def inner(left_operand, right_operand):
    return lax.dot_general(
        left_operand, right_operand, (((0,), (0,)), ((), ())), preferred_element_type=jnp.float32
    )


def against(left_operand, right_operand):
    return lax.dot_general(
        left_operand, right_operand, (((1,), (1,)), ((), ())), preferred_element_type=jnp.float32
    )


def norm_forward(values, gain):
    squares = lax.psum(jnp.sum(values * values, axis=1), "mp")
    rms = lax.rsqrt(squares / D + epsilon)[:, None]
    normed = (values * rms * gain).astype(jnp.bfloat16)
    return (rms, lax.all_gather(normed, "mp", axis=1, tiled=True))


def norm_backward(values, rms, gain, normed_grad):
    weighted = normed_grad * gain
    dotted = lax.psum(jnp.sum(weighted * values, axis=1), "mp")[:, None]
    grad = weighted * rms - values * (rms * rms * rms) * dotted / D
    gain_grad = jnp.sum(normed_grad * values * rms, axis=0)
    return (grad, gain_grad)


def spread_sum(terms):
    return lax.psum_scatter(
        terms.astype(jnp.bfloat16), "mp", scatter_dimension=1, tiled=True
    ).astype(jnp.float32)


def on_device(
    hidden_in,
    positions,
    head_counts,
    attention_gain,
    query_projection_weight,
    key_weight,
    value_weight,
    query_gain,
    key_gain,
    output_weight,
    feedforward_gain,
    gate_weight,
    up_weight,
    down_projection_weight,
    cotangent,
):
    parts = lax.axis_size("mp")
    rank = lax.axis_index("mp")
    tokens = hidden_in.shape[0]
    share = hidden_in.shape[1]
    slots_here = query_projection_weight.shape[1] // HD
    seqs = tokens // LEN
    scale = 1.0 / math.sqrt(HD)
    ranks = jnp.arange(parts, dtype=jnp.int32)
    offset = jnp.sum(jnp.where(ranks < rank, head_counts, 0))
    count = jnp.sum(jnp.where(ranks == rank, head_counts, 0))
    within = jnp.arange(slots_here, dtype=jnp.int32)
    live = (within < count).astype(jnp.float32)
    groups = jnp.minimum((offset + within) // (QH // KVH), KVH - 1)
    choose = (groups[:, None] == jnp.arange(KVH, dtype=jnp.int32)[None, :]).astype(jnp.float32)
    choose_low = choose.astype(jnp.bfloat16)
    cosine, sine = rotary_tables(positions)

    def turn(raw, gain):
        heads = raw.reshape(tokens, -1, HD)
        return rotate(head_norm(heads, gain), cosine[:, None, :], sine[:, None, :])

    inputs = hidden_in.astype(jnp.float32)
    first_rms, normed_full = norm_forward(inputs, attention_gain)
    queries = jnp.dot(normed_full, query_projection_weight, preferred_element_type=jnp.float32)
    keys = jnp.dot(normed_full, key_weight, preferred_element_type=jnp.float32)
    values_low = jnp.dot(normed_full, value_weight, preferred_element_type=jnp.float32).astype(
        jnp.bfloat16
    )
    turned_queries, query_pull = jax.vjp(turn, queries, query_gain)
    turned_keys, key_pull = jax.vjp(turn, keys, key_gain)
    turned_queries = turned_queries.astype(jnp.bfloat16)
    turned_keys = turned_keys.astype(jnp.bfloat16)
    query_heads = jnp.transpose(turned_queries.reshape(seqs, LEN, slots_here, HD), (0, 2, 1, 3))
    key_heads = jnp.einsum(
        "hg,slgd->shld",
        choose_low,
        turned_keys.reshape(seqs, LEN, KVH, HD),
        preferred_element_type=jnp.float32,
    ).astype(jnp.bfloat16)
    value_heads = jnp.einsum(
        "hg,slgd->shld",
        choose_low,
        values_low.reshape(seqs, LEN, KVH, HD),
        preferred_element_type=jnp.float32,
    ).astype(jnp.bfloat16)
    query_blocks = jnp.moveaxis(query_heads.reshape(seqs, slots_here, NBLK, BLK, HD), 2, 0)
    starts = jnp.arange(NBLK, dtype=jnp.int32) * BLK
    cols = jnp.arange(LEN, dtype=jnp.int32)

    def block_scores(block, start):
        scores = (
            jnp.einsum("shid,shjd->shij", block, key_heads, preferred_element_type=jnp.float32)
            * scale
        )
        rows = start + jnp.arange(BLK, dtype=jnp.int32)
        allowed = cols[None, :] <= rows[:, None]
        return jnp.where(allowed, scores, masked_score)

    def attend_block(block_args):
        block, start = block_args
        scores = block_scores(block, start)
        peak = jnp.max(scores, axis=-1, keepdims=True)
        weights = jnp.exp(scores - peak)
        total = jnp.sum(weights, axis=-1, keepdims=True)
        probs = (weights / total).astype(jnp.bfloat16)
        result = jnp.einsum(
            "shij,shjd->shid", probs, value_heads, preferred_element_type=jnp.float32
        )
        return (result, (peak + jnp.log(total))[..., 0])

    mixed, row_totals = lax.map(attend_block, (query_blocks, starts))
    mixed = jnp.moveaxis(mixed, 0, 2).reshape(seqs, slots_here, LEN, HD).astype(jnp.bfloat16)
    mixed = mixed * live.astype(jnp.bfloat16)[None, :, None, None]
    mixed_local = jnp.transpose(mixed, (0, 2, 1, 3)).reshape(tokens, slots_here * HD)
    all_heads = lax.all_gather(mixed_local, "mp", axis=1, tiled=True)
    branch = jnp.dot(all_heads, output_weight, preferred_element_type=jnp.float32)
    middle = inputs + branch
    second_rms, second_normed_complete = norm_forward(middle, feedforward_gain)
    gate = jnp.dot(second_normed_complete, gate_weight, preferred_element_type=jnp.float32)
    up = jnp.dot(second_normed_complete, up_weight, preferred_element_type=jnp.float32)
    sigma = jax.nn.sigmoid(gate)
    swish = gate * sigma
    hidden = (swish * up).astype(jnp.bfloat16)
    down_terms = jnp.dot(hidden, down_projection_weight, preferred_element_type=jnp.float32)
    output = (
        middle
        + lax.psum_scatter(
            down_terms.astype(jnp.bfloat16), "mp", scatter_dimension=1, tiled=True
        ).astype(jnp.float32)
    ).astype(jnp.bfloat16)
    cotangent_full = lax.all_gather(cotangent, "mp", axis=1, tiled=True)
    down_grad = inner(hidden, cotangent_full)
    hidden_grad = against(cotangent_full, down_projection_weight)
    gate_grad = (hidden_grad * up * sigma * (1.0 + gate * (1.0 - sigma))).astype(jnp.bfloat16)
    up_grad = (hidden_grad * swish).astype(jnp.bfloat16)
    gate_weight_grad = inner(second_normed_complete, gate_grad)
    up_weight_grad = inner(second_normed_complete, up_grad)
    normed_two_grad = spread_sum(against(gate_grad, gate_weight) + against(up_grad, up_weight))
    middle_part, feedforward_gain_grad = norm_backward(
        middle, second_rms, feedforward_gain, normed_two_grad
    )
    middle_grad = cotangent.astype(jnp.float32) + middle_part
    branch_grad = middle_grad.astype(jnp.bfloat16)
    output_weight_grad = inner(all_heads, branch_grad)
    slot_terms = against(branch_grad, output_weight)
    mixed_grad = lax.psum_scatter(
        slot_terms.astype(jnp.bfloat16), "mp", scatter_dimension=1, tiled=True
    ).astype(jnp.float32)
    mixed_grad = (mixed_grad.reshape(tokens, slots_here, HD) * live[None, :, None]).astype(
        jnp.bfloat16
    )
    grad_heads = jnp.transpose(mixed_grad.reshape(seqs, LEN, slots_here, HD), (0, 2, 1, 3))
    grad_blocks = jnp.moveaxis(grad_heads.reshape(seqs, slots_here, NBLK, BLK, HD), 2, 0)

    def back_block(carry, block_args):
        key_total, value_total = carry
        block, grad_block, row_total, start = block_args
        scores = block_scores(block, start)
        probs = jnp.exp(scores - row_total[..., None])
        probs_low = probs.astype(jnp.bfloat16)
        prob_grad = jnp.einsum(
            "shid,shjd->shij", grad_block, value_heads, preferred_element_type=jnp.float32
        )
        delta = jnp.sum(probs * prob_grad, axis=-1, keepdims=True)
        score_grad = (probs * (prob_grad - delta)).astype(jnp.bfloat16)
        query_grad = (
            jnp.einsum("shij,shjd->shid", score_grad, key_heads, preferred_element_type=jnp.float32)
            * scale
        )
        key_total = (
            key_total
            + jnp.einsum("shij,shid->shjd", score_grad, block, preferred_element_type=jnp.float32)
            * scale
        )
        value_total = value_total + jnp.einsum(
            "shij,shid->shjd", probs_low, grad_block, preferred_element_type=jnp.float32
        )
        return ((key_total, value_total), query_grad)

    empty = jnp.zeros((seqs, slots_here, LEN, HD), jnp.float32)
    (key_slot_grad, value_slot_grad), query_block_grads = lax.scan(
        back_block, (empty, empty), (query_blocks, grad_blocks, row_totals, starts)
    )
    query_rot_grad = jnp.moveaxis(query_block_grads, 0, 2).reshape(seqs, slots_here, LEN, HD)
    query_rot_grad = jnp.transpose(query_rot_grad, (0, 2, 1, 3)).reshape(tokens, slots_here, HD)
    key_rot_grad = jnp.einsum("hg,shld->slgd", choose, key_slot_grad).reshape(tokens, KVH, HD)
    value_grad = jnp.einsum("hg,shld->slgd", choose, value_slot_grad).reshape(tokens, KVH * HD)
    query_unrotated_gradient, query_gain_part = query_pull(query_rot_grad)
    key_raw_grad, key_gain_part = key_pull(key_rot_grad)
    summed = (
        lax.psum(key_raw_grad.astype(jnp.bfloat16), "mp").astype(jnp.float32),
        lax.psum(value_grad.astype(jnp.bfloat16), "mp").astype(jnp.float32),
        lax.psum(query_gain_part.astype(jnp.bfloat16), "mp").astype(jnp.float32),
        lax.psum(key_gain_part.astype(jnp.bfloat16), "mp").astype(jnp.float32),
    )
    keys_low = summed[0].astype(jnp.bfloat16)
    values_grad_low = summed[1].astype(jnp.bfloat16)
    queries_low = query_unrotated_gradient.astype(jnp.bfloat16)
    query_weight_grad = inner(normed_full, queries_low)
    key_weight_grad = inner(normed_full, keys_low)
    value_weight_grad = inner(normed_full, values_grad_low)
    normed_grad = spread_sum(against(queries_low, query_projection_weight))
    key_rows = lax.dynamic_slice_in_dim(key_weight, rank * share, share, 0)
    value_rows = lax.dynamic_slice_in_dim(value_weight, rank * share, share, 0)
    normed_grad = normed_grad + against(keys_low, key_rows) + against(values_grad_low, value_rows)
    input_part, attention_gain_grad = norm_backward(inputs, first_rms, attention_gain, normed_grad)
    input_gradient = middle_grad + input_part
    totals = (
        lax.psum(attention_gain_grad.astype(jnp.bfloat16), "dp").astype(jnp.float32),
        lax.psum(query_weight_grad.astype(jnp.bfloat16), "dp").astype(jnp.float32),
        lax.psum(key_weight_grad.astype(jnp.bfloat16), "dp").astype(jnp.float32),
        lax.psum(value_weight_grad.astype(jnp.bfloat16), "dp").astype(jnp.float32),
        lax.psum(summed[2].astype(jnp.bfloat16), "dp").astype(jnp.float32),
        lax.psum(summed[3].astype(jnp.bfloat16), "dp").astype(jnp.float32),
        lax.psum(output_weight_grad.astype(jnp.bfloat16), "dp").astype(jnp.float32),
        lax.psum(feedforward_gain_grad.astype(jnp.bfloat16), "dp").astype(jnp.float32),
        lax.psum(gate_weight_grad.astype(jnp.bfloat16), "dp").astype(jnp.float32),
        lax.psum(up_weight_grad.astype(jnp.bfloat16), "dp").astype(jnp.float32),
        lax.psum(down_grad.astype(jnp.bfloat16), "dp").astype(jnp.float32),
    )
    return (
        output,
        input_gradient,
        totals[0],
        totals[1],
        totals[2],
        totals[3],
        totals[4],
        totals[5],
        totals[6],
        totals[7],
        totals[8],
        totals[9],
        totals[10],
    )


def solution(mesh):
    in_specs = (
        P("dp", "mp"),
        P("dp"),
        P(),
        P("mp"),
        P(None, "mp"),
        P(),
        P(),
        P(),
        P(),
        P(None, "mp"),
        P("mp"),
        P(None, "mp"),
        P(None, "mp"),
        P("mp", None),
        P("dp", "mp"),
    )
    out_specs = (
        P("dp", "mp"),
        P("dp", "mp"),
        P("mp"),
        P(None, "mp"),
        P(),
        P(),
        P(),
        P(),
        P(None, "mp"),
        P("mp"),
        P(None, "mp"),
        P(None, "mp"),
        P("mp", None),
    )
    return jax.shard_map(
        on_device, mesh=mesh, in_specs=in_specs, out_specs=out_specs, check_vma=False
    )
```

profile of v0, /device:TPU:0, one launch (start us, length us, event | category | flops | bytes accessed | tf_op | source)
XLA Modules:
  0.0 2038.4 jit_solution(6352952060460513605)
XLA Ops:
  13.3 13.7 psum.133
  43.9 135.8 %all-gather.5.cloned.1.call-done = bf16[2048,2048]{0,1:T(8,128)(2,1)} async-done(((bf16[2048,512]{0,1:T(8,128)(2,1)}), bf16[2048,2048]{0,1:T(8,128)(2,1)}) %all-gather.5.cloned.1.call-update) | async-done | bytes 8388624 | tf_op jit(solution)/shard_map/all_gather | solution.py:53
  265.4 75.8 %while.30 = (s32[]{:T(128)}, bf16[2,2,6,512,64]{3,4,2,1,0:T(8,128)(2,1)}, f32[2,2,6,512]{3,2,1,0:T(8,128)S(1)}, s32[2]{0:T(128)S(1)}, bf16[2,2,6,512,64]{3,4,2,1...) while((s32[]{:T(128)}, ...), condition=%wide.region_8.9_spmd.clone.clone, body=%wide.region_5.8_spmd.clone.sunk.clone | while | flops 1686628864 | bytes 190279856 | solution.py:157
  347.0 113.7 %all-gather.7.cloned.1.call-done = bf16[2048,1536]{0,1:T(8,128)(2,1)} async-done(((bf16[2048,384]{0,1:T(8,128)(2,1)}), bf16[2048,1536]{0,1:T(8,128)(2,1)}) %all-gather.7.cloned.1.call-update) | async-done | bytes 6291472 | tf_op jit(solution)/shard_map/all_gather | solution.py:161
  482.3 148.5 %all-gather.9.cloned.1.call-done = bf16[2048,2048]{0,1:T(8,128)(2,1)} async-done(((bf16[2048,512]{0,1:T(8,128)(2,1)}), bf16[2048,2048]{0,1:T(8,128)(2,1)}) %all-gather.9.cloned.1.call-update) | async-done | bytes 8388624 | tf_op jit(solution)/shard_map/all_gather | solution.py:53
  630.8 14.9 fusion.109
  657.3 122.8 %all-gather.11.cloned.1.call-done = bf16[2048,2048]{1,0:T(8,128)(2,1)} async-done(((bf16[2048,512]{1,0:T(8,128)(2,1)}), bf16[2048,2048]{1,0:T(8,128)(2,1)}) %all-gather.11.cloned.1.call-update) | async-done | bytes 8388624 | tf_op jit(solution)/shard_map/all_gather | solution.py:177
  780.1 23.6 %multiply_convert_fusion.1 = (bf16[2048,1024]{1,0:T(8,128)(2,1)}, bf16[2048,1024]{1,0:T(8,128)(2,1)}, bf16[2048,1024]{1,0:T(8,128)(2,1)}) fusion(f32[2048,1024]{1,0:T(8,128)} %fusion.108, f32[2048,1024]{1,0:T(8,128)} %fusion.109, bf16[2048,2048]{1,0:T(8,128)(2,1)} %all-gather.11.cloned.1.call-done, bf16[1024,2048]{1,0:T(8,128)(2,1)} %param.32), kind=kOutput, calls=%fused_computation.53 | convolution fusion | flops 8621391872 | bytes 41943040 | tf_op jit(solution)/shard_map/dot_general | solution.py:44
  803.8 15.4 fusion.110
  819.2 14.4 add_convert_fusion
  833.6 14.0 convolution_convert_fusion.2
  851.6 124.8 %reduce-scatter.9.cloned.1.call-done = bf16[2048,512]{0,1:T(8,128)(2,1)} async-done(((bf16[2048,2048]{0,1:T(8,128)(2,1)}), bf16[2048,512]{0,1:T(8,128)(2,1)}) %reduce-scatter.9.cloned.1.call-update) | async-done | bytes 2097168 | tf_op jit(solution)/shard_map/reduce_scatter | solution.py:65
  992.7 131.9 %reduce-scatter.7.cloned.1.call-done = bf16[2048,512]{0,1:T(8,128)(2,1)} async-done(((bf16[2048,2048]{0,1:T(8,128)(2,1)}), bf16[2048,512]{0,1:T(8,128)(2,1)}) %reduce-scatter.7.cloned.1.call-update) | async-done | bytes 2097168 | tf_op jit(solution)/shard_map/reduce_scatter | solution.py:173
  1150.4 14.7 convolution_convert_fusion.3
  1193.4 64.9 %reduce-scatter.13.cloned.1.call-done = bf16[384,2048]{1,0:T(8,128)(2,1)} async-done(((bf16[1536,2048]{1,0:T(8,128)(2,1)}), bf16[384,2048]{1,0:T(8,128)(2,1)}) %reduce-scatter.13.cloned.1.call-update) | async-done | bytes 1572880
  1280.8 164.1 %while.31 = (s32[]{:T(128)}, f32[2,6,1024,64]{2,3,1,0:T(8,128)}, f32[2,6,1024,64]{2,3,1,0:T(8,128)}, f32[2,2,6,512,64]{3,4,2,1,0:T(8,128)}, s32[2]{0:T(128)S(1)}...) while((s32[]{:T(128)}, f32[2,6,1024,64]{2,3,1,0:T(8,128)}, ...), condition=%wide.region_19.20_spmd.clone.clone, body=%wide.region_17.19_spmd.clone.sunk.clone | while | flops 4125747712 | bytes 278057216 | solution.py:227
  1307.9 18.2 multiply_reduce_fusion.10
  1326.1 17.3 multiply_convert_fusion.8
  1374.9 14.3 select_add_fusion.7
  1389.2 18.2 multiply_reduce_fusion.10
  1407.4 17.3 multiply_convert_fusion.8
  1491.8 91.7 %all-reduce.13.cloned.1.call-done = (bf16[2048,320]{0,1:T(8,128)(2,1)}, bf16[2048,320]{0,1:T(8,128)(2,1)}) async-done(((bf16[2048,320]{0,1:T(8,128)(2,1)}, bf16[2048,320]{0,1:T(8,128)(2,1)}), (bf16[2048,320]{0,1:T(8,128)(2,1)}, bf16[2048,320]{0,1:T(8,128)(2,1)})) %all-reduce.13.cloned.1.call-update) | async-done | bytes 2621456 | tf_op jit(solution)/shard_map/psum | solution.py:237
  1625.4 210.8 %all-reduce.11.cloned.1.call-done = (bf16[2048,384]{1,0:T(8,128)(2,1)}, bf16[2048,320]{0,1:T(8,128)(2,1)}, bf16[2048,320]{0,1:T(8,128)(2,1)}, bf16[1536,512]{1,0...) async-done(((bf16[2048,384]{1,0:T(8,128)(2,1)}, bf16[2048,320]{0,1:T(8,128)(2,1)}, bf16[2048,320]{0,1:T(8,128)(2,1)}, ...) | async-done | bytes 18350096 | tf_op jit(solution)/shard_map/psum | solution.py:256
  1860.1 122.8 %reduce-scatter.11.cloned.1.call-done = bf16[2048,512]{0,1:T(8,128)(2,1)} async-done(((bf16[2048,2048]{0,1:T(8,128)(2,1)}), bf16[2048,512]{0,1:T(8,128)(2,1)}) %reduce-scatter.11.cloned.1.call-update) | async-done | bytes 2097168 | tf_op jit(solution)/shard_map/reduce_scatter | solution.py:65
  (340 shorter events, 557.9 us)
Async XLA Ops:
  7.2 218.1 %copy-start = (bf16[2048,384]{1,0:T(8,128)(2,1)S(1)}, bf16[2048,384]{1,0:T(8,128)(2,1)}, u32[]{:S(2)}) copy-start(bf16[2048,384]{1,0:T(8,128)(2,1)} %param.23) | copy-start | bytes 4718596
  7.2 172.6 %all-gather.5.cloned.1.call-start = ((), (), s32[]{:S(2)}) async-start(), calls=%async_computation.4 | async-start | bytes 10485760 | tf_op jit(solution)/shard_map/all_gather | solution.py:53
  31.7 148.1 %copy-start.43 = (bf16[2048,320]{0,1:T(8,128)(2,1)S(1)}, bf16[2048,320]{0,1:T(8,128)(2,1)}, u32[]{:S(2)}) copy-start(bf16[2048,320]{0,1:T(8,128)(2,1)} %param.25) | copy-start | bytes 3932164
  31.7 429.0 %all-gather.7.cloned.1.call-start = ((), (), s32[]{:S(2)}) async-start(), calls=%async_computation.5 | async-start | bytes 7864320 | tf_op jit(solution)/shard_map/all_gather | solution.py:161
  31.9 155.3 %copy-start.58 = (f32[32]{0:T(128)}, f32[32]{0:T(128)S(1)}, u32[]{:S(2)}) copy-start(f32[32]{0:T(128)S(1)} %multiply_exponential_fusion) | copy-start | bytes 388
  33.2 189.5 %copy-start.50 = (s32[6]{0:T(128)}, s32[6]{0:T(128)S(1)}, u32[]{:S(2)}) copy-start(s32[6]{0:T(128)S(1)} %fusion.101) | copy-start | bytes 76
  42.6 173.4 %copy-start.16 = (f32[2,1024,64]{1,0,2:T(2,128)}, f32[2,1024,64]{1,0,2:T(2,128)S(1)}, u32[]{:S(2)}) copy-start(f32[2,1024,64]{1,0,2:T(2,128)S(1)} %get-tuple-element.371) | copy-start | bytes 1572868
  305.2 24.5 %copy-start.9 = (bf16[2,6,1024,64]{2,3,1,0:T(8,128)(2,1)S(1)}, bf16[2,6,1024,64]{2,3,1,0:T(8,128)(2,1)}, u32[]{:S(2)}) copy-start(bf16[2,6,1024,64]{2,3,1,0:T(8,128)(2,1)} %get-tuple-element.557) | copy-start | bytes 4718596 | tf_op jit(solution)/shard_map/while
  345.3 115.4 %copy-start.67 = (bf16[1536,512]{1,0:T(8,128)(2,1)S(1)}, bf16[1536,512]{1,0:T(8,128)(2,1)}, u32[]{:S(2)}) copy-start(bf16[1536,512]{1,0:T(8,128)(2,1)} %param.28) | copy-start | bytes 4718596
  347.0 130.8 %copy-start.47 = (f32[512]{0:T(512)S(1)}, f32[512]{0:T(512)}, u32[]{:S(2)}) copy-start(f32[512]{0:T(512)} %param.29) | copy-start | bytes 6148
  347.0 283.8 %all-gather.9.cloned.1.call-start = ((), (), s32[]{:S(2)}) async-start(), calls=%async_computation.6 | async-start | bytes 10485760 | tf_op jit(solution)/shard_map/all_gather | solution.py:53
  481.7 298.4 %all-gather.11.cloned.1.call-start = ((), (), s32[]{:S(2)}) async-start(), calls=%async_computation.8 | async-start | bytes 10485760 | tf_op jit(solution)/shard_map/all_gather | solution.py:177
  482.3 494.1 %reduce-scatter.9.cloned.1.call-start = ((), (), s32[]{:S(2)}) async-start(), calls=%async_computation.9 | async-start | bytes 10485760 | tf_op jit(solution)/shard_map/reduce_scatter | solution.py:65
  833.6 291.0 %reduce-scatter.7.cloned.1.call-start = ((), (), s32[]{:S(2)}) async-start(), calls=%async_computation.7 | async-start | bytes 10485760 | tf_op jit(solution)/shard_map/reduce_scatter | solution.py:173
  847.7 410.7 %reduce-scatter.13.cloned.1.call-start = ((), (), s32[]{:S(2)}) async-start(), calls=%async_computation.11 | async-start | bytes 7864320
  1146.7 436.8 %all-reduce.13.cloned.1.call-start = ((), (), s32[]{:S(2)}) async-start(), calls=%async_computation.13 | async-start | bytes 5242880 | tf_op jit(solution)/shard_map/psum | solution.py:237
  1150.4 27.5 %slice-start.4 = ((s8[8388608]{0:T(1024)(128)(4,1)}), s8[4194304]{0:T(1024)(128)(4,1)S(1)}, s32[]{:S(2)}) async-start(s8[8388608]{0:T(1024)(128)(4,1)} %bitcast.239), calls=%async_computation.18 | async-start | bytes 8388608
  1478.3 357.9 %all-reduce.11.cloned.1.call-start = ((), (), s32[]{:S(2)}) async-start(), calls=%async_computation.12 | async-start | bytes 36700160 | tf_op jit(solution)/shard_map/psum | solution.py:256
  1598.8 384.1 %reduce-scatter.11.cloned.1.call-start = ((), (), s32[]{:S(2)}) async-start(), calls=%async_computation.10 | async-start | bytes 10485760 | tf_op jit(solution)/shard_map/reduce_scatter | solution.py:65
  1855.6 127.3 %copy-start.33 = (bf16[2048,320]{0,1:T(8,128)(2,1)S(1)}, bf16[2048,320]{0,1:T(8,128)(2,1)}, u32[]{:S(2)}) copy-start(bf16[2048,320]{0,1:T(8,128)(2,1)} %get-tuple-element.349) | copy-start | bytes 3932164
  1855.6 127.3 %copy-start.41 = (f32[2048]{0:T(1024)S(1)}, f32[2048]{0:T(1024)}, u32[]{:S(2)}) copy-start(f32[2048]{0:T(1024)} %copy-done.40) | copy-start | bytes 24580
  1855.6 127.3 %copy-start.49 = (f32[512]{0:T(512)S(1)}, f32[512]{0:T(512)}, u32[]{:S(2)}) copy-start(f32[512]{0:T(512)} %param.22) | copy-start | bytes 6148
  1860.1 130.7 %copy-start.57 = (bf16[512]{0:T(512)(128)(2,1)S(1)}, bf16[512]{0:T(512)(128)(2,1)}, u32[]{:S(2)}) copy-start(bf16[512]{0:T(512)(128)(2,1)} %get-tuple-element.291) | copy-start | bytes 3076
  1860.1 158.0 %copy-start.46 = (f32[2048]{0:T(1024)S(1)}, f32[2048]{0:T(1024)}, u32[]{:S(2)}) copy-start(f32[2048]{0:T(1024)} %get-tuple-element.373) | copy-start | bytes 24580
  (73 other events, 500.6 us)
Sparse Core Ops, SparseCore 0:
  31.9 147.8 all-gather.4
  347.1 113.5 all-gather.6
  481.8 148.9 all-gather.8
  632.2 147.8 all-gather.10
  833.7 142.6 reduce-scatter.8
  979.2 145.3 reduce-scatter.6
  1146.8 111.4 reduce-scatter.12
  1478.4 105.0 all-reduce.12
  1598.9 237.2 all-reduce.10
  1838.4 144.4 reduce-scatter.10
where the time goes:
time: 2050 us; the launch traced here: 2040 us
  waiting for transfers between devices  1270 us (62%)
  matrix products  376 us (18%)
  other arithmetic  173 us (8%)
  local copies, waits for them, and re-layouts  134 us (7%)
  blocking collectives  69.5 us (3%)
    all_gather x2, waiting for transfers between devices, norm_forward(): return (rms, lax.all_gather(normed, 'mp', axis=1, tiled=True))  284 us
    reduce_scatter x2, waiting for transfers between devices, spread_sum(): lax.psum_scatter(terms.astype(jnp.bfloat16), 'mp', scatter_dimension=1, t...  248 us
    psum x1, waiting for transfers between devices, on_device(): lax.psum(query_weight_grad.astype(jnp.bfloat16), 'dp').astype(jnp.float32)  211 us
    reduce_scatter x1, waiting for transfers between devices, on_device(): lax.psum_scatter(down_terms.astype(jnp.bfloat16), 'mp', scatter_dimension...  132 us
    all_gather x1, waiting for transfers between devices, on_device(): cotangent_full = lax.all_gather(cotangent, 'mp', axis=1, tiled=True)  123 us
    all_gather x1, waiting for transfers between devices, on_device(): all_heads = lax.all_gather(mixed_local, 'mp', axis=1, tiled=True)  114 us
    psum x1, waiting for transfers between devices, on_device(): lax.psum(key_raw_grad.astype(jnp.bfloat16), 'mp').astype(jnp.float32)  91.7 us
    dot_general x7, matrix products, against(): lax.dot_general(left_operand, right_operand, (((1,), (1,)), ((), ())), pr...  77.7 us
  transfers between devices with their start and end apart: 10, of which 10 were waited for; matrix products, arithmetic and copies ran while one was open for 8% of the time, Pallas kernels for 0%

commit v1 on v0

--- a/solution.py
+++ b/solution.py
@@ -233,8 +233,9 @@
     value_grad = jnp.einsum("hg,shld->slgd", choose, value_slot_grad).reshape(tokens, KVH * HD)
     query_unrotated_gradient, query_gain_part = query_pull(query_rot_grad)
     key_raw_grad, key_gain_part = key_pull(key_rot_grad)
+    recast_copies_over_axis = lambda local: jnp.sum(lax.all_gather(local, "mp"), 0)
     summed = (
-        lax.psum(key_raw_grad.astype(jnp.bfloat16), "mp").astype(jnp.float32),
+        recast_copies_over_axis(key_raw_grad.astype(jnp.bfloat16)).astype(jnp.float32),
         lax.psum(value_grad.astype(jnp.bfloat16), "mp").astype(jnp.float32),
         lax.psum(query_gain_part.astype(jnp.bfloat16), "mp").astype(jnp.float32),
         lax.psum(key_gain_part.astype(jnp.bfloat16), "mp").astype(jnp.float32),

time: 2050 us -> 2050 us (level)
    psum x1, waiting for transfers between devices: 91.7 us -> 0.01 us  [on_device(): lax.psum(value_grad.astype(jnp.bfloat16), 'mp').astype(jnp.float32)]
    all_gather x0 -> x1, waiting for transfers between devices: none -> 67.5 us  [on_device(): lax.all_gather(local, 'mp')]
    unnamed x11 -> x12, waiting for transfers between devices: 65.6 us -> 109 us
    unnamed x162 -> x146, local copies, waits for them, and re-layouts: 52.8 us -> 49.7 us
  transfers between devices with their start and end apart: 10 -> 11, of which waited for: 10 -> 10; matrix products, arithmetic and copies ran while one was open for 8% -> 10% of each run, Pallas kernels for 0% -> 0%
where the time goes in v1:
time: 2050 us; the launch traced here: 2030 us
  waiting for transfers between devices  1270 us (62%)
  matrix products  378 us (18%)
  other arithmetic  174 us (8%)
  local copies, waits for them, and re-layouts  129 us (6%)
  blocking collectives  69.4 us (3%)
    all_gather x2, waiting for transfers between devices, norm_forward(): return (rms, lax.all_gather(normed, 'mp', axis=1, tiled=True))  284 us
    reduce_scatter x2, waiting for transfers between devices, spread_sum(): lax.psum_scatter(terms.astype(jnp.bfloat16), 'mp', scatter_dimension=1, t...  242 us
    psum x1, waiting for transfers between devices, on_device(): lax.psum(query_weight_grad.astype(jnp.bfloat16), 'dp').astype(jnp.float32)  196 us
    reduce_scatter x1, waiting for transfers between devices, on_device(): lax.psum_scatter(down_terms.astype(jnp.bfloat16), 'mp', scatter_dimension...  132 us
    all_gather x1, waiting for transfers between devices, on_device(): cotangent_full = lax.all_gather(cotangent, 'mp', axis=1, tiled=True)  123 us
    all_gather x1, waiting for transfers between devices, on_device(): all_heads = lax.all_gather(mixed_local, 'mp', axis=1, tiled=True)  114 us
    unnamed x12, waiting for transfers between devices  109 us
    dot_general x7, matrix products, against(): lax.dot_general(left_operand, right_operand, (((1,), (1,)), ((), ())), pr...  78.1 us
  transfers between devices with their start and end apart: 11, of which 10 were waited for; matrix products, arithmetic and copies ran while one was open for 10% of the time, Pallas kernels for 0%

profile of v1, /device:TPU:0, one launch (start us, length us, event | category | flops | bytes accessed | tf_op | source)
XLA Modules:
  0.0 2034.2 jit_solution(8335228176183180837)
XLA Ops:
  44.0 135.8 %all-gather.6.cloned.1.call-done = bf16[2048,2048]{0,1:T(8,128)(2,1)} async-done(((bf16[2048,512]{0,1:T(8,128)(2,1)}), bf16[2048,2048]{0,1:T(8,128)(2,1)}) %all-gather.6.cloned.1.call-update) | async-done | bytes 8388624 | tf_op jit(solution)/shard_map/all_gather | solution.py:53
  265.4 75.7 %while.30 = (s32[]{:T(128)}, bf16[2,2,6,512,64]{3,4,2,1,0:T(8,128)(2,1)}, f32[2,2,6,512]{3,2,1,0:T(8,128)S(1)}, s32[2]{0:T(128)S(1)}, bf16[2,2,6,512,64]{3,4,2,1...) while((s32[]{:T(128)}, ...), condition=%wide.region_8.9_spmd.clone.clone, body=%wide.region_5.8_spmd.clone.sunk.clone | while | flops 1686628864 | bytes 190279856 | solution.py:157
  346.8 113.7 %all-gather.8.cloned.1.call-done = bf16[2048,1536]{0,1:T(8,128)(2,1)} async-done(((bf16[2048,384]{0,1:T(8,128)(2,1)}), bf16[2048,1536]{0,1:T(8,128)(2,1)}) %all-gather.8.cloned.1.call-update) | async-done | bytes 6291472 | tf_op jit(solution)/shard_map/all_gather | solution.py:161
  482.1 148.5 %all-gather.10.cloned.1.call-done = bf16[2048,2048]{0,1:T(8,128)(2,1)} async-done(((bf16[2048,512]{0,1:T(8,128)(2,1)}), bf16[2048,2048]{0,1:T(8,128)(2,1)}) %all-gather.10.cloned.1.call-update) | async-done | bytes 8388624 | tf_op jit(solution)/shard_map/all_gather | solution.py:53
  630.6 14.9 fusion.109
  657.1 122.8 %all-gather.12.cloned.1.call-done = bf16[2048,2048]{1,0:T(8,128)(2,1)} async-done(((bf16[2048,512]{1,0:T(8,128)(2,1)}), bf16[2048,2048]{1,0:T(8,128)(2,1)}) %all-gather.12.cloned.1.call-update) | async-done | bytes 8388624 | tf_op jit(solution)/shard_map/all_gather | solution.py:177
  779.9 23.7 %multiply_convert_fusion.1 = (bf16[2048,1024]{1,0:T(8,128)(2,1)}, bf16[2048,1024]{1,0:T(8,128)(2,1)}, bf16[2048,1024]{1,0:T(8,128)(2,1)}) fusion(f32[2048,1024]{1,0:T(8,128)} %fusion.108, f32[2048,1024]{1,0:T(8,128)} %fusion.109, bf16[2048,2048]{1,0:T(8,128)(2,1)} %all-gather.12.cloned.1.call-done, bf16[1024,2048]{1,0:T(8,128)(2,1)} %param.32), kind=kOutput, calls=%fused_computation.53 | convolution fusion | flops 8621391872 | bytes 41943040 | tf_op jit(solution)/shard_map/dot_general | solution.py:44
  803.7 15.3 fusion.110
  819.0 14.4 add_convert_fusion
  833.4 14.0 convolution_convert_fusion.2
  851.4 124.8 %reduce-scatter.9.cloned.1.call-done = bf16[2048,512]{0,1:T(8,128)(2,1)} async-done(((bf16[2048,2048]{0,1:T(8,128)(2,1)}), bf16[2048,512]{0,1:T(8,128)(2,1)}) %reduce-scatter.9.cloned.1.call-update) | async-done | bytes 2097168 | tf_op jit(solution)/shard_map/reduce_scatter | solution.py:65
  992.5 131.9 %reduce-scatter.7.cloned.1.call-done = bf16[2048,512]{0,1:T(8,128)(2,1)} async-done(((bf16[2048,2048]{0,1:T(8,128)(2,1)}), bf16[2048,512]{0,1:T(8,128)(2,1)}) %reduce-scatter.7.cloned.1.call-update) | async-done | bytes 2097168 | tf_op jit(solution)/shard_map/reduce_scatter | solution.py:173
  1150.0 108.2 %reduce-scatter.13.cloned.1.call-done = bf16[384,2048]{1,0:T(8,128)(2,1)} async-done(((bf16[1536,2048]{1,0:T(8,128)(2,1)}), bf16[384,2048]{1,0:T(8,128)(2,1)}) %reduce-scatter.13.cloned.1.call-update) | async-done | bytes 1572880
  1280.7 164.2 %while.31 = (s32[]{:T(128)}, f32[2,6,1024,64]{2,3,1,0:T(8,128)}, f32[2,6,1024,64]{2,3,1,0:T(8,128)}, f32[2,2,6,512,64]{3,4,2,1,0:T(8,128)}, s32[2]{0:T(128)S(1)}...) while((s32[]{:T(128)}, f32[2,6,1024,64]{2,3,1,0:T(8,128)}, ...), condition=%wide.region_19.20_spmd.clone.clone, body=%wide.region_17.19_spmd.clone.sunk.clone | while | flops 4125747712 | bytes 278057216 | solution.py:227
  1307.6 18.2 multiply_reduce_fusion.10
  1325.7 17.3 multiply_convert_fusion.8
  1374.6 14.3 select_add_fusion.7
  1388.9 18.2 multiply_reduce_fusion.10
  1407.0 17.3 multiply_convert_fusion.8
  1486.3 14.7 convolution_convert_fusion.3
  1544.8 67.5 %all-gather.14.cloned.1.call-done = bf16[4,2048,320]{1,2,0:T(8,128)(2,1)} async-done(((bf16[1,2048,320]{1,2,0:T(8,128)(2,1)}), bf16[4,2048,320]{1,2,0:T(8,128)(2,1)}) %all-gather.14.cloned.1.call-update) | async-done | bytes 5242896 | tf_op jit(solution)/shard_map/all_gather | solution.py:236
  1641.2 116.9 %reduce-scatter.11.cloned.1.call-done = bf16[2048,512]{0,1:T(8,128)(2,1)} async-done(((bf16[2048,2048]{0,1:T(8,128)(2,1)}), bf16[2048,512]{0,1:T(8,128)(2,1)}) %reduce-scatter.11.cloned.1.call-update) | async-done | bytes 2097168 | tf_op jit(solution)/shard_map/reduce_scatter | solution.py:65
  1766.4 13.8 all-reduce.4
  1807.8 195.9 %all-reduce.12.cloned.1.call-done = (bf16[2048,384]{1,0:T(8,128)(2,1)}, bf16[2048,320]{0,1:T(8,128)(2,1)}, bf16[2048,320]{0,1:T(8,128)(2,1)}, bf16[1536,512]{1,0...) async-done(((bf16[2048,384]{1,0:T(8,128)(2,1)}, bf16[2048,320]{0,1:T(8,128)(2,1)}, bf16[2048,320]{0,1:T(8,128)(2,1)}, ...) | async-done | bytes 18350096 | tf_op jit(solution)/shard_map/psum | solution.py:257
  (328 shorter events, 556.1 us)
Async XLA Ops:
  7.2 218.0 %copy-start = (bf16[2048,384]{1,0:T(8,128)(2,1)S(1)}, bf16[2048,384]{1,0:T(8,128)(2,1)}, u32[]{:S(2)}) copy-start(bf16[2048,384]{1,0:T(8,128)(2,1)} %param.23) | copy-start | bytes 4718596
  7.2 172.6 %all-gather.6.cloned.1.call-start = ((), (), s32[]{:S(2)}) async-start(), calls=%async_computation.4 | async-start | bytes 10485760 | tf_op jit(solution)/shard_map/all_gather | solution.py:53
  31.7 148.1 %copy-start.36 = (bf16[2048,320]{0,1:T(8,128)(2,1)S(1)}, bf16[2048,320]{0,1:T(8,128)(2,1)}, u32[]{:S(2)}) copy-start(bf16[2048,320]{0,1:T(8,128)(2,1)} %param.25) | copy-start | bytes 3932164
  31.7 428.8 %all-gather.8.cloned.1.call-start = ((), (), s32[]{:S(2)}) async-start(), calls=%async_computation.5 | async-start | bytes 7864320 | tf_op jit(solution)/shard_map/all_gather | solution.py:161
  31.9 155.2 %copy-start.51 = (f32[32]{0:T(128)}, f32[32]{0:T(128)S(1)}, u32[]{:S(2)}) copy-start(f32[32]{0:T(128)S(1)} %multiply_exponential_fusion) | copy-start | bytes 388
  33.2 189.4 %copy-start.43 = (s32[6]{0:T(128)}, s32[6]{0:T(128)S(1)}, u32[]{:S(2)}) copy-start(s32[6]{0:T(128)S(1)} %fusion.101) | copy-start | bytes 76
  42.6 173.3 %copy-start.14 = (f32[2,1024,64]{1,0,2:T(2,128)}, f32[2,1024,64]{1,0,2:T(2,128)S(1)}, u32[]{:S(2)}) copy-start(f32[2,1024,64]{1,0,2:T(2,128)S(1)} %get-tuple-element.369) | copy-start | bytes 1572868
  345.1 115.4 %copy-start.60 = (bf16[1536,512]{1,0:T(8,128)(2,1)S(1)}, bf16[1536,512]{1,0:T(8,128)(2,1)}, u32[]{:S(2)}) copy-start(bf16[1536,512]{1,0:T(8,128)(2,1)} %param.28) | copy-start | bytes 4718596
  346.8 130.8 %copy-start.40 = (f32[512]{0:T(512)S(1)}, f32[512]{0:T(512)}, u32[]{:S(2)}) copy-start(f32[512]{0:T(512)} %param.29) | copy-start | bytes 6148
  346.8 283.8 %all-gather.10.cloned.1.call-start = ((), (), s32[]{:S(2)}) async-start(), calls=%async_computation.6 | async-start | bytes 10485760 | tf_op jit(solution)/shard_map/all_gather | solution.py:53
  481.5 298.4 %all-gather.12.cloned.1.call-start = ((), (), s32[]{:S(2)}) async-start(), calls=%async_computation.8 | async-start | bytes 10485760 | tf_op jit(solution)/shard_map/all_gather | solution.py:177
  482.1 494.1 %reduce-scatter.9.cloned.1.call-start = ((), (), s32[]{:S(2)}) async-start(), calls=%async_computation.9 | async-start | bytes 10485760 | tf_op jit(solution)/shard_map/reduce_scatter | solution.py:65
  833.4 291.0 %reduce-scatter.7.cloned.1.call-start = ((), (), s32[]{:S(2)}) async-start(), calls=%async_computation.7 | async-start | bytes 10485760 | tf_op jit(solution)/shard_map/reduce_scatter | solution.py:173
  847.4 410.8 %reduce-scatter.13.cloned.1.call-start = ((), (), s32[]{:S(2)}) async-start(), calls=%async_computation.13 | async-start | bytes 7864320
  1146.6 390.5 %all-reduce.10.cloned.1.call-start = ((), (), s32[]{:S(2)}) async-start(), calls=%async_computation.12 | async-start | bytes 2621440 | tf_op jit(solution)/shard_map/psum | solution.py:239
  1280.7 164.3 %copy-start.44 = (s32[6]{0:T(128)S(1)}, s32[6]{0:T(128)}, u32[]{:S(2)}) copy-start(s32[6]{0:T(128)} %copy-done.43) | copy-start | bytes 76
  1451.7 160.6 %all-gather.14.cloned.1.call-start = ((), (), s32[]{:S(2)}) async-start(), calls=%async_computation.11 | async-start | bytes 6553600 | tf_op jit(solution)/shard_map/all_gather | solution.py:236
  1472.0 286.2 %reduce-scatter.11.cloned.1.call-start = ((), (), s32[]{:S(2)}) async-start(), calls=%async_computation.10 | async-start | bytes 10485760 | tf_op jit(solution)/shard_map/reduce_scatter | solution.py:65
  1486.2 517.6 %all-reduce.12.cloned.1.call-start = ((), (), s32[]{:S(2)}) async-start(), calls=%async_computation.14 | async-start | bytes 36700160 | tf_op jit(solution)/shard_map/psum | solution.py:257
  1501.0 30.5 %slice-start.2 = ((s8[8388608]{0:T(1024)(128)(4,1)}), s8[4194304]{0:T(1024)(128)(4,1)S(1)}, s32[]{:S(2)}) async-start(s8[8388608]{0:T(1024)(128)(4,1)} %bitcast.237), calls=%async_computation.17 | async-start | bytes 8388608
  1636.9 121.2 %copy-start.34 = (f32[2048]{0:T(1024)S(1)}, f32[2048]{0:T(1024)}, u32[]{:S(2)}) copy-start(f32[2048]{0:T(1024)} %copy-done.33) | copy-start | bytes 24580
  1636.9 121.2 %copy-start.42 = (f32[512]{0:T(512)S(1)}, f32[512]{0:T(512)}, u32[]{:S(2)}) copy-start(f32[512]{0:T(512)} %param.22) | copy-start | bytes 6148
  1641.2 125.1 %copy-start.50 = (bf16[512]{0:T(512)(128)(2,1)S(1)}, bf16[512]{0:T(512)(128)(2,1)}, u32[]{:S(2)}) copy-start(bf16[512]{0:T(512)(128)(2,1)} %get-tuple-element.291) | copy-start | bytes 3076
  1641.2 152.9 %copy-start.39 = (f32[2048]{0:T(1024)S(1)}, f32[2048]{0:T(1024)}, u32[]{:S(2)}) copy-start(f32[2048]{0:T(1024)} %get-tuple-element.371) | copy-start | bytes 24580
  (66 other events, 518.1 us)
Sparse Core Ops, SparseCore 0:
  31.9 147.8 all-gather.5
  346.9 113.5 all-gather.7
  481.6 148.9 all-gather.9
  632.0 147.8 all-gather.11
  833.5 142.6 reduce-scatter.8
  979.0 145.3 reduce-scatter.6
  1146.7 111.4 reduce-scatter.12
  1451.8 60.5 all-reduce.9
  1514.5 97.7 all-gather.13
  1615.1 143.0 reduce-scatter.10
  1764.6 239.1 all-reduce.11
